TPU v7x, 32 devices: a whole 2x2x4 slice. The times are simulated.
32 devices in a mesh: ctx: 8 (over z, x), tp: 4 (over y, core).
Axes of the slice: x: 2, y: 2, z: 4, core: 2. Of those that a mesh axis runs over, the one named last changes fastest.
Arguments:
- query_branch: bfloat16 [2048, 8192], P('ctx', 'tp'), may hold values from -6 to 6
- key_branch: bfloat16 [2048, 8192], P('ctx', 'tp'), may hold values from -6 to 6
- value_branch: bfloat16 [2048, 8192], P('ctx', 'tp'), may hold values from -6 to 6
- out_cotangent: bfloat16 [2048, 8192], P('ctx', 'tp'), may hold values from -6 to 6
- out_weight: bfloat16 [8192, 8192], P('tp', 'ctx'), may hold values from -0.09375 to 0.09375
- residues: float32 [512, 16], P('tp'), may hold values from -1.5 to 1.5
- decay_rates: float32 [512, 16], P('tp'), may hold values from 4.93164063e-05 to 0.0799
- skip_gains: float32 [8192], P('tp'), may hold values from 0.1 to 1.9
- record_lengths: int32 [24], replicated, may hold values from 1 to 512, 2048 in all
Outputs:
- block_output: bfloat16 [2048, 8192], P('ctx', 'tp')
- query_grad: bfloat16 [2048, 8192], P('ctx', 'tp')
- key_grad: bfloat16 [2048, 8192], P('ctx', 'tp')
- value_grad: bfloat16 [2048, 8192], P('ctx', 'tp')
Inputs may be any that keep to these rules, and one draw needn't show every extreme that they name: record_lengths sum to 2048; the longest record has exactly 512 tokens.
All inputs are finite; a program needn't handle non-finite values.
Results may differ from a plain program's by a relative error of at most 0.006.
Values may be sent and summed in bfloat16 or wider, within the bound.
A program may use at most 128 MiB of HBM per device.

v0:
```python
import math

import jax
import jax.numpy as jnp
from jax import lax
from jax.sharding import PartitionSpec as P

GSIZE = 16


highest = lax.Precision.HIGHEST
triple = lax.Precision.HIGH


def record_starts(lengths_in, positions):
    offsets = jnp.cumsum(lengths_in) - lengths_in
    return jnp.max((positions[:, None] == offsets[None, :]).astype(jnp.float32), axis=1)


def edge_terms(rates, coeffs, start_flags):
    length = start_flags.shape[0]
    position = jnp.arange(length, dtype=jnp.float32)
    segment = jnp.cumsum(start_flags)
    decay_pow = jnp.exp(-rates[None, :, :] * position[:, None, None])
    first_seg = (segment == 0).astype(jnp.float32)[:, None, None]
    last_seg = (segment == segment[-1]).astype(jnp.float32)[:, None, None]
    inflow = coeffs[None] * decay_pow * jnp.exp(-rates)[None] * first_seg
    outflow = jnp.exp(-rates[None] * (length - 1.0 - position)[:, None, None]) * last_seg
    through = (jnp.exp(-rates * length) * (segment[-1] == 0).astype(jnp.float32)).T
    return (segment, decay_pow, inflow, outflow, through)


def block_kernel(rates, coeffs, segment, decay_pow):
    length = segment.shape[0]
    position = jnp.arange(length, dtype=jnp.float32)
    growth = jnp.exp(rates[None] * position[:, None, None])
    keep_mask = (
        (position[:, None] >= position[None, :]) & (segment[:, None] == segment[None, :])
    ).astype(jnp.float32)
    kernel = jnp.einsum("tgn,sgn->gts", coeffs[None] * decay_pow, growth, precision=triple)
    return kernel * keep_mask[None]


def forward_run(values, rates, coeffs, start_flags):
    length, groups, width = values.shape
    block_len = min(length, 512)
    num_blocks = length // block_len

    def forward_one_block(carried, inputs):
        section, flags_here = inputs
        segment, decay_pow, inflow, outflow, through = edge_terms(rates, coeffs, flags_here)
        kernel = block_kernel(rates, coeffs, segment, decay_pow)
        result = jnp.einsum("gts,sgj->tgj", kernel, section, precision=triple)
        result = result + jnp.einsum("tgn,ngj->tgj", inflow, carried, precision=highest)
        carried = (
            jnp.einsum("sgn,sgj->ngj", outflow, section, precision=highest)
            + through[:, :, None] * carried
        )
        return (carried, result)

    initial = jnp.zeros((rates.shape[1], groups, width), jnp.float32)
    carried, results = lax.scan(
        forward_one_block,
        initial,
        (
            values.reshape(num_blocks, block_len, groups, width),
            start_flags.reshape(num_blocks, block_len),
        ),
    )
    return (results.reshape(length, groups, width), carried)


def adjoint_run(values, rates, coeffs, start_flags):
    length, groups, width = values.shape
    block_len = min(length, 512)
    num_blocks = length // block_len

    def adjoint_one_block(carried, inputs):
        section, flags_here = inputs
        segment, decay_pow, inflow, outflow, through = edge_terms(rates, coeffs, flags_here)
        kernel = block_kernel(rates, coeffs, segment, decay_pow)
        result = jnp.einsum("gts,tgj->sgj", kernel, section, precision=triple)
        result = result + jnp.einsum("sgn,ngj->sgj", outflow, carried, precision=highest)
        carried = (
            jnp.einsum("tgn,tgj->ngj", inflow, section, precision=highest)
            + through[:, :, None] * carried
        )
        return (carried, result)

    initial = jnp.zeros((rates.shape[1], groups, width), jnp.float32)
    carried, results = lax.scan(
        adjoint_one_block,
        initial,
        (
            values.reshape(num_blocks, block_len, groups, width),
            start_flags.reshape(num_blocks, block_len),
        ),
        reverse=True,
    )
    return (results.reshape(length, groups, width), carried)


def by_groups(runner, values, rates, coeffs, start_flags):
    length, groups, width = values.shape
    group_block = math.gcd(groups, 8)
    num_sets = groups // group_block
    value_sets = values.reshape(length, num_sets, group_block, width).transpose(1, 0, 2, 3)
    rate_sets = rates.reshape(num_sets, group_block, rates.shape[1])
    coeff_sets = coeffs.reshape(num_sets, group_block, coeffs.shape[1])

    def run_set(operands):
        return runner(operands[0], operands[1], operands[2], start_flags)

    results, carried = lax.map(run_set, (value_sets, rate_sets, coeff_sets))
    results = results.transpose(1, 0, 2, 3).reshape(length, groups, width)
    carried = carried.transpose(1, 0, 2, 3).reshape(rates.shape[1], groups, width)
    return (results, carried)


def on_device(
    query_branch,
    key_branch,
    value_branch,
    out_cotangent,
    out_weight,
    residues,
    decay_rates,
    skip_gains,
    record_lengths,
):
    tok_rows, channels = query_branch.shape
    groups = channels // GSIZE
    coeffs = residues * jnp.sqrt(1.0 - jnp.exp(-2.0 * decay_rates))
    gated = (key_branch.astype(jnp.float32) * value_branch.astype(jnp.float32)).astype(jnp.bfloat16)
    dev_index = lax.axis_index("ctx")
    ctx_devices = lax.axis_size("ctx")
    seq_flags = record_starts(record_lengths, jnp.arange(tok_rows * ctx_devices, dtype=jnp.int32))

    def group_params(group_share):
        rates_here = lax.dynamic_slice_in_dim(decay_rates, dev_index * group_share, group_share, 0)
        coeffs_here = lax.dynamic_slice_in_dim(coeffs, dev_index * group_share, group_share, 0)
        return (rates_here, coeffs_here)

    received = lax.all_to_all(
        gated.reshape(tok_rows, groups, GSIZE), "ctx", split_axis=1, concat_axis=0, tiled=True
    )
    rates_here, coeffs_here = group_params(received.shape[1])
    filt_here, unused = by_groups(
        forward_run, received.astype(jnp.float32), rates_here, coeffs_here, seq_flags
    )
    filtered = lax.all_to_all(
        filt_here.astype(jnp.bfloat16), "ctx", split_axis=0, concat_axis=1, tiled=True
    )
    filtered = lax.optimization_barrier(filtered.reshape(tok_rows, channels)).astype(jnp.float32)
    mixed = filtered + skip_gains[None, :] * gated.astype(jnp.float32)
    mixer_out = (query_branch.astype(jnp.float32) * mixed).astype(jnp.bfloat16)
    cot_full = lax.all_gather(out_cotangent, "tp", axis=1, tiled=True)
    w_piece = lax.all_gather(out_weight, "ctx", axis=1, tiled=True)
    partial_out = jnp.dot(mixer_out, w_piece, preferred_element_type=jnp.float32)
    back_sum = lax.dot_general(
        cot_full, w_piece, (((1,), (1,)), ((), ())), preferred_element_type=jnp.float32
    )
    partial_out, back_sum = (partial_out, back_sum)
    block_output = lax.psum_scatter(partial_out, "tp", scatter_dimension=1, tiled=True).astype(
        jnp.bfloat16
    )
    mixer_grad = lax.optimization_barrier(back_sum.astype(jnp.bfloat16)).astype(jnp.float32)
    filter_grad = (mixer_grad * query_branch.astype(jnp.float32)).astype(jnp.bfloat16)
    query_grad = (mixer_grad * mixed).astype(jnp.bfloat16)
    received = lax.all_to_all(
        filter_grad.reshape(tok_rows, groups, GSIZE), "ctx", split_axis=1, concat_axis=0, tiled=True
    )
    rates_here, coeffs_here = group_params(received.shape[1])
    adj_here, unused = by_groups(
        adjoint_run, received.astype(jnp.float32), rates_here, coeffs_here, seq_flags
    )
    adjoint_sum = lax.all_to_all(
        adj_here.astype(jnp.bfloat16), "ctx", split_axis=0, concat_axis=1, tiled=True
    )
    adjoint_sum = lax.optimization_barrier(adjoint_sum.reshape(tok_rows, channels)).astype(
        jnp.float32
    )
    gated_grad = adjoint_sum + skip_gains[None, :] * filter_grad.astype(jnp.float32)
    key_grad = (gated_grad * value_branch.astype(jnp.float32)).astype(jnp.bfloat16)
    value_grad = (gated_grad * key_branch.astype(jnp.float32)).astype(jnp.bfloat16)
    return (block_output, query_grad, key_grad, value_grad)


def solution(mesh):
    placed = (
        P("ctx", "tp"),
        P("ctx", "tp"),
        P("ctx", "tp"),
        P("ctx", "tp"),
        P("tp", "ctx"),
        P("tp", None),
        P("tp", None),
        P("tp"),
        P(),
    )
    return jax.shard_map(
        on_device,
        mesh=mesh,
        in_specs=placed,
        out_specs=(P("ctx", "tp"), P("ctx", "tp"), P("ctx", "tp"), P("ctx", "tp")),
        check_vma=False,
    )
```

profile of v0, /device:TPU:4, one launch (start us, length us, event | category | flops | bytes accessed | tf_op | source)
XLA Modules:
  0.0 1225.5 jit_solution(7314100662254278369)
XLA Ops:
  8.7 35.4 %all-gather.5.cloned.1.call-done = bf16[256,8192]{1,0:T(8,128)(2,1)} async-done(((bf16[256,2048]{1,0:T(8,128)(2,1)}), bf16[256,8192]{1,0:T(8,128)(2,1)}) %all-gather.5.cloned.1.call-update) | async-done | bytes 4194320 | tf_op jit(solution)/shard_map/all_gather | solution.py:157
  44.1 640.4 %all-gather.3.cloned.1.call-done = bf16[2048,8192]{1,0:T(8,128)(2,1)} async-done(((bf16[2048,1024]{1,0:T(8,128)(2,1)}), bf16[2048,8192]{1,0:T(8,128)(2,1)}) %all-gather.3.cloned.1.call-update) | async-done | bytes 33554448 | tf_op jit(solution)/shard_map/all_gather | solution.py:158
  684.5 15.7 %convolution_convert_fusion = bf16[256,2048]{1,0:T(8,128)(2,1)S(1)} fusion(bf16[256,8192]{1,0:T(8,128)(2,1)} %all-gather.5.cloned.1.call-done, bf16[2048,8192]{1,0:T(8,128)(2,1)} %all-gather.3.cloned.1.call-done), kind=kOutput, calls=%fused_computation.108 | convolution fusion | flops 8590458880 | bytes 38797312 | tf_op jit(solution)/shard_map/dot_general | solution.py:160
  701.9 5.1 all-to-all-start.2
  707.7 25.2 %all-to-all-done.2 = bf16[256,128,16]{0,2,1:T(8,128)(2,1)S(1)} async-done(((bf16[256,128,16]{0,2,1:T(8,128)(2,1)}), bf16[256,128,16]{0,2,1:T(8,128)(2,1)S(1)}, u32[]{:S(2)}, u32[]{:S(2)}) %all-to-all-start.2) | async-done | bytes 1048608 | tf_op jit(solution)/shard_map/all_to_all | solution.py:170
  736.5 107.7 %while.75 = (s32[]{:T(128)}, bf16[2,2048,8,16]{1,3,2,0:T(8,128)(2,1)S(1)}, f32[2,2048,8,16]{1,3,2,0:T(8,128)}, f32[2048]{0:T(1024)}, f32[2,8,16]{2,1,0:T(8,128)S...) while((s32[]{:T(128)}, ...), condition=%wide.wide.region_14.15_spmd, body=%wide.wide.region_9.14_spmd.sunk | while | flops 431762432 | bytes 27981396 | solution.py:114
  738.8 51.1 %while.77 = (s32[]{:T(128)}, f32[16,8,16]{0,2,1:T(8,128)S(1)}, bf16[4,512,8,16]{1,0,3,2:T(4,128)(2,1)S(1)}, f32[4,512,8,16]{1,0,3,2:T(4,128)S(1)}, f32[8,16]{1,0...) while((s32[]{:T(128)}, f32[16,8,16]{0,2,1:T(8,128)S(1)}, ...), condition=%wide.region_13.13_spmd.clone, body=%wide.region_10.12_spmd.clone.sunk | while | flops 431762176 | bytes 21161280 | solution.py:91
  740.9 4.0 fusion.114
  745.1 2.4 fusion.116
  748.2 2.1 dynamic_update_slice.39
  753.7 4.0 fusion.114
  757.9 2.4 fusion.116
  766.5 4.0 fusion.114
  770.7 2.4 fusion.116
  779.3 4.0 fusion.114
  783.5 2.4 fusion.116
  786.6 2.1 dynamic_update_slice.39
  792.6 51.1 %while.77 = (s32[]{:T(128)}, f32[16,8,16]{0,2,1:T(8,128)S(1)}, bf16[4,512,8,16]{1,0,3,2:T(4,128)(2,1)S(1)}, f32[4,512,8,16]{1,0,3,2:T(4,128)S(1)}, f32[8,16]{1,0...) while((s32[]{:T(128)}, f32[16,8,16]{0,2,1:T(8,128)S(1)}, ...), condition=%wide.region_13.13_spmd.clone, body=%wide.region_10.12_spmd.clone.sunk | while | flops 431762176 | bytes 21161280 | solution.py:91
  794.8 4.0 fusion.114
  799.0 2.4 fusion.116
  802.1 2.1 dynamic_update_slice.39
  807.5 4.0 fusion.114
  811.8 2.4 fusion.116
  814.9 2.1 dynamic_update_slice.39
  820.3 4.0 fusion.114
  824.6 2.4 fusion.116
  833.1 4.0 fusion.114
  837.4 2.4 fusion.116
  844.3 8.7 copy.69
  852.9 10.4 reshape.425
  863.4 29.3 %all_to_all.48 = bf16[8,2,32768]{2,1,0:T(2,128)(2,1)S(1)} all-to-all(bf16[8,2,32768]{2,1,0:T(2,128)(2,1)S(1)} %reshape.425), channel_id=1, replica_groups=mesh['ctx'=8,'tp'=4] {'ctx'}, dimensions={0} | all-to-all | bytes 2097152 | tf_op jit(solution)/shard_map/all_to_all | solution.py:177
  892.7 7.5 reshape.426
  900.3 8.8 copy.71
  910.3 3.9 fusion.69
  915.5 3.6 all-to-all-start
  919.2 25.5 %all-to-all-done = bf16[256,128,16]{0,2,1:T(8,128)(2,1)S(1)} async-done(((bf16[256,128,16]{0,2,1:T(8,128)(2,1)}), bf16[256,128,16]{0,2,1:T(8,128)(2,1)S(1)}, u32[]{:S(2)}, u32[]{:S(2)}) %all-to-all-start) | async-done | bytes 1048608 | tf_op jit(solution)/shard_map/all_to_all | solution.py:144
  948.4 115.1 %while.73 = (s32[]{:T(128)}, bf16[2,2048,8,16]{1,3,2,0:T(8,128)(2,1)S(1)}, f32[2,2048,8,16]{1,3,2,0:T(8,128)}, f32[2048]{0:T(1024)}, f32[2,8,16]{2,1,0:T(8,128)S...) while((s32[]{:T(128)}, ...), condition=%wide.wide.region_7.8_spmd, body=%wide.wide.region_2.7_spmd.sunk | while | flops 431762432 | bytes 27457060 | solution.py:114
  950.6 55.0 %while.76 = (s32[]{:T(128)}, f32[16,8,16]{0,2,1:T(8,128)S(1)}, bf16[4,512,8,16]{1,0,3,2:T(4,128)(2,1)S(1)}, f32[4,512,8,16]{1,0,3,2:T(4,128)S(1)}, f32[1,8,16]{2...) while((s32[]{:T(128)}, f32[16,8,16]{0,2,1:T(8,128)S(1)}, ...), condition=%wide.region_6.6_spmd.clone, body=%wide.region_3.5_spmd.clone.sunk | while | flops 431762176 | bytes 21161260 | solution.py:62
  951.4 4.0 fusion.124
  955.7 3.4 fusion.126
  959.8 2.1 dynamic_update_slice.40
  965.2 4.0 fusion.124
  969.4 3.4 fusion.126
  978.9 4.0 fusion.124
  983.2 3.4 fusion.126
  992.7 4.0 fusion.124
  996.9 3.4 fusion.126
  1008.1 55.0 %while.76 = (s32[]{:T(128)}, f32[16,8,16]{0,2,1:T(8,128)S(1)}, bf16[4,512,8,16]{1,0,3,2:T(4,128)(2,1)S(1)}, f32[4,512,8,16]{1,0,3,2:T(4,128)S(1)}, f32[1,8,16]{2...) while((s32[]{:T(128)}, f32[16,8,16]{0,2,1:T(8,128)S(1)}, ...), condition=%wide.region_6.6_spmd.clone, body=%wide.region_3.5_spmd.clone.sunk | while | flops 431762176 | bytes 21161260 | solution.py:62
  1009.0 4.0 fusion.124
  1013.2 3.4 fusion.126
  1022.7 4.0 fusion.124
  1027.0 3.4 fusion.126
  1036.5 4.0 fusion.124
  1040.7 3.4 fusion.126
  1050.2 4.0 fusion.124
  1054.5 3.4 fusion.126
  1063.6 8.5 copy.63
  1072.1 10.4 reshape.423
  1082.5 29.1 %all_to_all.49 = bf16[8,2,32768]{2,1,0:T(2,128)(2,1)S(1)} all-to-all(bf16[8,2,32768]{2,1,0:T(2,128)(2,1)S(1)} %reshape.423), channel_id=1, replica_groups=mesh['ctx'=8,'tp'=4] {'ctx'}, dimensions={0} | all-to-all | bytes 2097152 | tf_op jit(solution)/shard_map/all_to_all | solution.py:151
  1111.7 7.5 reshape.424
  1119.2 8.8 copy.65
  1129.2 17.3 %fusion.74 = f32[256,8192]{1,0:T(8,128)} fusion(bf16[2048,8192]{1,0:T(8,128)(2,1)} %all-gather.3.cloned.1.call-done, bf16[256,2048]{1,0:T(8,128)(2,1)} %param.17, bf16[256,2048]{1,0:T(8,128)(2,1)S(1)} %copy-done.3, bf16[256,2048]{1,0:T(8,128)(2,1)S(1)} %copy.66, f32[2048]{0:T(1024)S(1)} %copy-done.10), kind=kOutput, calls=%fused_computation.119 | convolution fusion | flops 8593604608 | bytes 45096960 | tf_op jit(solution)/shard_map/dot_general | solution.py:159
  1149.3 66.7 %reduce-scatter.2.cloned.1.call-done = f32[256,2048]{1,0:T(8,128)} async-done(((f32[256,8192]{1,0:T(8,128)}), f32[256,2048]{1,0:T(8,128)}) %reduce-scatter.2.cloned.1.call-update) | async-done | bytes 2097168 | tf_op jit(solution)/shard_map/reduce_scatter | solution.py:164
  1216.0 2.7 convert_element_type.184
  (345 shorter events, 108.2 us)
Async XLA Ops:
  7.2 36.9 %all-gather.5.cloned.1.call-start = ((), (), s32[]{:S(2)}) async-start(), calls=%async_computation.7 | async-start | bytes 5242880 | tf_op jit(solution)/shard_map/all_gather | solution.py:157
  7.9 676.6 %all-gather.3.cloned.1.call-start = ((), (), s32[]{:S(2)}) async-start(), calls=%async_computation.5 | async-start | bytes 37748736 | tf_op jit(solution)/shard_map/all_gather | solution.py:158
  8.6 691.5 %copy-start.6 = (bf16[256,2048]{1,0:T(8,128)(2,1)S(1)}, bf16[256,2048]{1,0:T(8,128)(2,1)}, u32[]{:S(2)}) copy-start(bf16[256,2048]{1,0:T(8,128)(2,1)} %param.17) | copy-start | bytes 3145732
  700.2 1.8 copy-start.4
  700.6 1.4 copy-start
  700.6 6.5 copy-start.11
  700.6 6.5 copy-start.12
  700.6 6.7 copy-start.13
  701.9 31.0 %all-to-all-start.2 = ((bf16[256,128,16]{0,2,1:T(8,128)(2,1)}), bf16[256,128,16]{0,2,1:T(8,128)(2,1)S(1)}, u32[]{:S(2)}, u32[]{:S(2)}) async-start(bf16[256,128,16]{0,2,1:T(8,128)(2,1)} %bitcast.19), calls=%async_computation.3 | async-start | bytes 2097152 | tf_op jit(solution)/shard_map/all_to_all | solution.py:170
  707.7 25.3 %copy-start.7 = (f32[2048]{0:T(1024)}, f32[2048]{0:T(1024)S(1)}, u32[]{:S(2)}) copy-start(f32[2048]{0:T(1024)S(1)} %convert_reduce_fusion) | copy-start | bytes 24580
  909.1 1.2 copy-start.1
  909.1 1.2 copy-start.9
  914.1 1.3 copy-start.2
  914.2 5.0 copy-start.8
  915.5 29.2 %all-to-all-start = ((bf16[256,128,16]{0,2,1:T(8,128)(2,1)}), bf16[256,128,16]{0,2,1:T(8,128)(2,1)S(1)}, u32[]{:S(2)}, u32[]{:S(2)}) async-start(bf16[256,128,16]{0,2,1:T(8,128)(2,1)} %bitcast.6), calls=%async_computation | async-start | bytes 2097152 | tf_op jit(solution)/shard_map/all_to_all | solution.py:144
  919.1 296.9 %reduce-scatter.2.cloned.1.call-start = ((), (), s32[]{:S(2)}) async-start(), calls=%async_computation.6 | async-start | bytes 10485760 | tf_op jit(solution)/shard_map/reduce_scatter | solution.py:164
  1128.0 1.2 copy-start.3
  1128.0 1.2 copy-start.10
  1146.6 1.2 copy-start.5
Sparse Core Ops, SparseCore 0:
  9.5 34.5 all-gather.4
  45.6 638.7 all-gather.2
  1146.7 69.2 reduce-scatter.1
where the time goes:
time: 1230 us
  waiting for transfers between devices  795 us (65%)
  matrix products  159 us (13%)
  local copies, waits for them, and re-layouts  149 us (12%)
  blocking collectives  58.5 us (5%)
  other arithmetic  30.1 us (2%)
  between operations  14.3 us (1%)
    all_gather x1, waiting for transfers between devices, on_device(): w_piece = lax.all_gather(out_weight, 'ctx', axis=1, tiled=True)  640 us
    reduce_scatter x1, waiting for transfers between devices, on_device(): lax.psum_scatter(partial_out, 'tp', scatter_dimension=1, tiled=True)  66.7 us
    dot_general x16, matrix products, block_kernel(): jnp.einsum('tgn,sgn->gts', coeffs[None] * decay_pow, growth, precision=tr...  63.4 us
    unnamed x32, local copies, waits for them, and re-layouts  38.3 us
    dynamic_update_slice x32, local copies, waits for them, and re-layouts, forward_run(): lax.scan(forward_one_block, initial, (values.reshape(num_blocks, block_le...  37 us
    all_gather x1, waiting for transfers between devices, on_device(): cot_full = lax.all_gather(out_cotangent, 'tp', axis=1, tiled=True)  35.4 us
    all_to_all x1, blocking collectives, on_device(): lax.all_to_all(adj_here.astype(jnp.bfloat16), 'ctx', split_axis=0, concat...  29.3 us
    all_to_all x1, blocking collectives, on_device(): lax.all_to_all(filt_here.astype(jnp.bfloat16), 'ctx', split_axis=0, conca...  29.1 us
  transfers between devices with their start and end apart: 5, of which 5 were waited for; matrix products, arithmetic and copies ran while one was open for 0% of the time, Pallas kernels for 0%

commit v1 on v0

v1 whole, which is shorter than its diff:
```python
import functools

import jax
import jax.numpy as jnp
from jax import lax
from jax.experimental import pallas as pl
from jax.experimental.pallas import tpu as pltpu
from jax.sharding import Mesh, PartitionSpec as P

GSIZE = 16
LANES = 128
TILE_GROUPS = LANES // GSIZE
F32, BF16 = jnp.float32, jnp.bfloat16


def split(a):
    hi = a.astype(BF16)
    return hi, (a - hi.astype(F32)).astype(BF16)


def wide(block, length):
    return jnp.concatenate([block[...]] * (length // LANES), axis=1)


def positions(rows, length):
    return lax.broadcasted_iota(jnp.int32, (rows, length), 1).astype(F32)


def inflow_rows(rates, coeffs, pos, first):
    return coeffs * jnp.exp(-rates * (pos + 1.0)) * first


def outflow_rows(rates, pos, last):
    return jnp.exp(-rates * (pos.shape[1] - 1.0 - pos)) * last


def own_lanes(shape, group):
    lane = lax.broadcasted_iota(jnp.int32, shape, 1)
    return (lane >= group * GSIZE) & (lane < (group + 1) * GSIZE)


def weighted_state(rows, x, modes):
    hi, lo = split(rows)
    full = jnp.dot(hi, x, preferred_element_type=F32) + jnp.dot(lo, x, preferred_element_type=F32)
    state = jnp.zeros((modes, LANES), F32)
    for g in range(TILE_GROUPS):
        part = full[g * modes : (g + 1) * modes]
        state = jnp.where(own_lanes(part.shape, g), part, state)
    return state


def contract_first(a, b):
    return lax.dot_general(a, b, (((0,), (0,)), ((), ())), preferred_element_type=F32)


def from_state(rows, state, modes):
    blocks = [
        jnp.where(own_lanes(state.shape, g), state, 0.0) for g in range(TILE_GROUPS)
    ]
    state_rows = jnp.concatenate(blocks, axis=0)
    r_hi, r_lo = split(rows)
    s_hi, s_lo = split(state_rows)
    return contract_first(r_hi, s_hi) + contract_first(r_lo, s_hi) + contract_first(r_hi, s_lo)


def convolve(left, right, mask, x, modes):
    l_hi, l_lo = split(left)
    r_hi, r_lo = split(right)
    total = jnp.zeros(x.shape, F32)
    for g in range(TILE_GROUPS):
        rows = slice(g * modes, (g + 1) * modes)
        a = jnp.concatenate([l_hi[rows], l_lo[rows], l_hi[rows]], axis=0)
        b = jnp.concatenate([r_hi[rows], r_hi[rows], r_lo[rows]], axis=0)
        kernel = (contract_first(a, b) * mask).astype(BF16)
        part = jnp.dot(kernel, x, preferred_element_type=F32)
        total = jnp.where(own_lanes(x.shape, g), part, total)
    return total


def gated_of(key, value):
    return (key[...].astype(F32) * value[...].astype(F32)).astype(BF16)


def forward_state(modes, key, value, rates, last, out):
    length = key.shape[0]
    pos = positions(rates.shape[0], length)
    rows = outflow_rows(wide(rates, length), pos, last[...])
    out[...] = weighted_state(rows, gated_of(key, value), modes)


def forward_filter(modes, key, value, query, skip, rates, coeffs, first, mask, state, mixed, mixer):
    length = key.shape[0]
    pos = positions(rates.shape[0], length)
    r, c = wide(rates, length), wide(coeffs, length)
    x = gated_of(key, value)
    half = length / 2.0
    left = c * jnp.exp(-r * (pos - half))
    right = jnp.exp(r * (pos - half))
    total = convolve(left, right, mask[...], x, modes)
    total = total + from_state(inflow_rows(r, c, pos, first[...]), state[...], modes)
    result = total.astype(BF16).astype(F32) + skip[...] * x.astype(F32)
    mixed[...] = result
    mixer[...] = (query[...].astype(F32) * result).astype(BF16)


def adjoint_state(modes, grad, query, mixed, rates, coeffs, first, filter_grad, query_grad, out):
    length = grad.shape[0]
    pos = positions(rates.shape[0], length)
    r, c = wide(rates, length), wide(coeffs, length)
    g = grad[...].astype(F32)
    f = (g * query[...].astype(F32)).astype(BF16)
    filter_grad[...] = f
    query_grad[...] = (g * mixed[...]).astype(BF16)
    out[...] = weighted_state(inflow_rows(r, c, pos, first[...]), f, modes)


def adjoint_filter(modes, grad, key, value, skip, rates, coeffs, last, mask, state, key_grad, value_grad):
    length = grad.shape[0]
    pos = positions(rates.shape[0], length)
    r, c = wide(rates, length), wide(coeffs, length)
    f = grad[...]
    half = length / 2.0
    left = jnp.exp(r * (pos - half))
    right = c * jnp.exp(-r * (pos - half))
    total = convolve(left, right, mask[...], f, modes)
    total = total + from_state(outflow_rows(r, pos, last[...]), state[...], modes)
    result = total.astype(BF16).astype(F32) + skip[...] * f.astype(F32)
    key_grad[...] = (result * value[...].astype(F32)).astype(BF16)
    value_grad[...] = (result * key[...].astype(F32)).astype(BF16)


def tiled_call(body, modes, kinds, operands, outs, length, channels, flops):
    rows = TILE_GROUPS * modes
    specs = {
        "tok": pl.BlockSpec((length, LANES), lambda i: (0, i)),
        "par": pl.BlockSpec((rows, LANES), lambda i: (i, 0)),
        "row": pl.BlockSpec((1, length), lambda i: (0, 0)),
        "skip": pl.BlockSpec((1, LANES), lambda i: (0, i)),
        "mask": pl.BlockSpec((length, length), lambda i: (0, 0)),
        "state": pl.BlockSpec((modes, LANES), lambda i: (0, i)),
    }
    shapes = {"tok": (length, channels), "state": (modes, channels)}
    moved = sum(o.size * o.dtype.itemsize for o in operands)
    return pl.pallas_call(
        functools.partial(body, modes),
        grid=(channels // LANES,),
        in_specs=[specs[k] for k in kinds],
        out_specs=[specs[k] for k, _ in outs],
        out_shape=[jax.ShapeDtypeStruct(shapes[k], d) for k, d in outs],
        cost_estimate=pl.CostEstimate(flops=flops, bytes_accessed=moved, transcendentals=0),
    )(*operands)


def on_device(
    query_branch,
    key_branch,
    value_branch,
    out_cotangent,
    out_weight,
    residues,
    decay_rates,
    skip_gains,
    record_lengths,
):
    length, channels = query_branch.shape
    modes = residues.shape[1]
    nz, nx, ntp = lax.axis_size("z"), lax.axis_size("x"), lax.axis_size("tp")
    ctx = nz * nx
    hops = -(-(length * ctx // 4) // length)
    index = lax.axis_index("z") * nx + lax.axis_index("x")

    transposed = [
        ((z * nx + x) * ntp + t, (t * nx + x) * ntp + z)
        for z in range(nz)
        for x in range(nx)
        for t in range(ntp)
    ]
    cot = lax.ppermute(out_cotangent, ("z", "x", "tp"), transposed)
    cot_all = lax.all_gather(cot, "tp", axis=0, tiled=True)
    weight = lax.all_gather(out_weight, "x", axis=1, tiled=True)

    offsets = jnp.cumsum(record_lengths) - record_lengths
    everywhere = jnp.arange(length * ctx, dtype=jnp.int32)
    starts = jnp.any(everywhere[:, None] == offsets[None, :], axis=1).astype(jnp.int32)
    starts = starts.reshape(ctx, length)
    closed = jnp.max(starts, axis=1)
    flags = lax.dynamic_index_in_dim(starts, index, 0, keepdims=False)
    segment = jnp.cumsum(flags)
    first = (segment == 0).astype(F32)[None, :]
    last = (segment == segment[-1]).astype(F32)[None, :]
    at = jnp.arange(length)
    mask = ((at[:, None] >= at[None, :]) & (segment[:, None] == segment[None, :])).astype(F32)

    coeffs = residues * jnp.sqrt(1.0 - jnp.exp(-2.0 * decay_rates))
    rates_rows = jnp.broadcast_to(decay_rates.reshape(-1, 1), (decay_rates.size, LANES))
    coeff_rows = jnp.broadcast_to(coeffs.reshape(-1, 1), (coeffs.size, LANES))
    through = jnp.repeat(jnp.exp(-decay_rates * length).T, GSIZE, axis=1)
    skip = skip_gains[None, :]
    tiles = channels // LANES
    conv_flops = tiles * TILE_GROUPS * 2 * length * length * 512
    state_flops = tiles * 2 * 256 * 256 * length

    def gathered_state(state, direction):
        total = jnp.zeros_like(state)
        factor = jnp.ones_like(state)
        for hop in range(1, hops + 1):
            pairs = [
                (c, c + direction * hop) for c in range(ctx) if 0 <= c + direction * hop < ctx
            ]
            total = total + factor * lax.ppermute(state, ("z", "x"), pairs)
            passed = jnp.clip(index - direction * hop, 0, ctx - 1)
            open_here = 1.0 - closed[passed].astype(F32)
            factor = factor * through * open_here
        return total

    (own,) = tiled_call(
        forward_state, modes, ("tok", "tok", "par", "row"),
        (key_branch, value_branch, rates_rows, last),
        (("state", F32),), length, channels, state_flops,
    )
    entering = gathered_state(own, 1)
    mixed, mixer_out = tiled_call(
        forward_filter, modes,
        ("tok", "tok", "tok", "skip", "par", "par", "row", "mask", "state"),
        (key_branch, value_branch, query_branch, skip, rates_rows, coeff_rows, first, mask, entering),
        (("tok", F32), ("tok", BF16)), length, channels, conv_flops,
    )
    mixer_all = lax.all_gather(mixer_out, "z", axis=0, tiled=True)

    back = lax.dot_general(
        cot_all, weight, (((1,), (1,)), ((), ())), preferred_element_type=F32
    ).astype(BF16)
    mixer_grad = lax.psum_scatter(back, "z", scatter_dimension=0, tiled=True)
    partial = jnp.dot(mixer_all, weight, preferred_element_type=F32).astype(BF16)
    summed = lax.psum_scatter(partial, "tp", scatter_dimension=0, tiled=True)
    block_output = lax.ppermute(summed, ("z", "x", "tp"), transposed)

    filter_grad, query_grad, own = tiled_call(
        adjoint_state, modes, ("tok", "tok", "tok", "par", "par", "row"),
        (mixer_grad, query_branch, mixed, rates_rows, coeff_rows, first),
        (("tok", BF16), ("tok", BF16), ("state", F32)), length, channels, state_flops,
    )
    entering = gathered_state(own, -1)
    key_grad, value_grad = tiled_call(
        adjoint_filter, modes,
        ("tok", "tok", "tok", "skip", "par", "par", "row", "mask", "state"),
        (filter_grad, key_branch, value_branch, skip, rates_rows, coeff_rows, last, mask.T, entering),
        (("tok", BF16), ("tok", BF16)), length, channels, conv_flops,
    )
    return (block_output, query_grad, key_grad, value_grad)


def solution(mesh):
    ctx, tp = mesh.devices.shape
    fine = Mesh(mesh.devices.reshape(tp, ctx // tp, tp), ("z", "x", "tp"))
    tokens = P(("z", "x"), "tp")
    placed = (
        tokens,
        tokens,
        tokens,
        tokens,
        P("tp", ("z", "x")),
        P("tp", None),
        P("tp", None),
        P("tp"),
        P(),
    )
    return jax.shard_map(
        on_device,
        mesh=fine,
        in_specs=placed,
        out_specs=(tokens, tokens, tokens, tokens),
        check_vma=False,
    )
```

time: 1230 us -> 469 us (0.38)
  waiting for transfers between devices: 795 us -> 335 us
  local copies, waits for them, and re-layouts: 149 us -> 8.31 us
  matrix products: 159 us -> 27.7 us
  blocking collectives: 58.5 us -> 0 us
  Pallas kernels: 0 us -> 56.9 us
  other arithmetic: 30.1 us -> 4.4 us
    all_gather x2 -> x3, waiting for transfers between devices: 676 us -> 163 us  [the longest x1 93.9 us: on_device(): weight = lax.all_gather(out_weight, 'x', axis=1, tiled=True)]
    dot_general x66 -> x2, matrix products: 159 us -> 27.7 us  [the longest x1 13.9 us: on_device(): lax.dot_general(cot_all, weight, (((1,), (1,)), ((), ())), preferred_elem...]
    ppermute x0 -> x6, waiting for transfers between devices: none -> 76 us  [the longest x1 47.5 us: on_device(): cot = lax.ppermute(out_cotangent, ('z', 'x', 'tp'), transposed)]
    all_to_all x2 -> x0, blocking collectives: 58.5 us -> none  [the longest x1 29.3 us: on_device(): lax.all_to_all(adj_here.astype(jnp.bfloat16), 'ctx', split_axis=0, concat...]
    pallas_call x0 -> x4, Pallas kernels: none -> 56.9 us  [tiled_call(): pl.pallas_call(functools.partial(body, modes), grid=(channels // LANES,),...]
    all_to_all x2 -> x0, waiting for transfers between devices: 50.7 us -> none  [the longest x1 25.5 us: on_device(): lax.all_to_all(gated.reshape(tok_rows, groups, GSIZE), 'ctx', split_axis=...]
    dynamic_update_slice x36 -> x0, local copies, waits for them, and re-layouts: 37.3 us -> none  [the longest x32 37 us: forward_run(): lax.scan(forward_one_block, initial, (values.reshape(num_blocks, block_le...]
    unnamed x32 -> x10, local copies, waits for them, and re-layouts: 38.3 us -> 2.05 us
  transfers between devices with their start and end apart: 5 -> 11, of which waited for: 5 -> 6; matrix products, arithmetic and copies ran while one was open for 0% -> 8% of each run, Pallas kernels for 0% -> 12%
where the time goes in v1:
time: 469 us; the launch traced here: 465 us
  waiting for transfers between devices  335 us (71%)
  Pallas kernels  56.9 us (12%)
  matrix products  27.7 us (6%)
  starting transfers between devices  18 us (4%)
  between operations  15.2 us (3%)
  local copies, waits for them, and re-layouts  8.31 us (2%)
    all_gather x1, waiting for transfers between devices, on_device(): weight = lax.all_gather(out_weight, 'x', axis=1, tiled=True)  93.9 us
    all_gather x1, waiting for transfers between devices, on_device(): mixer_all = lax.all_gather(mixer_out, 'z', axis=0, tiled=True)  69 us
    reduce_scatter x1, waiting for transfers between devices, on_device(): mixer_grad = lax.psum_scatter(back, 'z', scatter_dimension=0, tiled=True)  63.6 us
    pallas_call x4, Pallas kernels, tiled_call(): pl.pallas_call(functools.partial(body, modes), grid=(channels // LANES,),...  56.9 us
    ppermute x1, waiting for transfers between devices, on_device(): cot = lax.ppermute(out_cotangent, ('z', 'x', 'tp'), transposed)  47.5 us
    reduce_scatter x1, waiting for transfers between devices, on_device(): summed = lax.psum_scatter(partial, 'tp', scatter_dimension=0, tiled=True)  31.5 us
    ppermute x1, waiting for transfers between devices, on_device(): block_output = lax.ppermute(summed, ('z', 'x', 'tp'), transposed)  28.5 us
    dot_general x1, matrix products, on_device(): lax.dot_general(cot_all, weight, (((1,), (1,)), ((), ())), preferred_elem...  13.9 us
  transfers between devices with their start and end apart: 11, of which 6 were waited for; matrix products, arithmetic and copies ran while one was open for 8% of the time, Pallas kernels for 12%

profile of v1, /device:TPU:4, one launch (start us, length us, event | category | flops | bytes accessed | tf_op | source)
XLA Modules:
  0.0 465.3 jit_solution(11668455350152612648)
XLA Ops:
  7.2 0.0 copy-start.3
  7.2 0.0 copy-start.1
  7.2 0.0 all-gather.8.cloned.1.call-start
  7.2 4.4 collective-permute-start.3
  11.7 47.5 %collective-permute-done.3 = bf16[256,2048]{1,0:T(8,128)(2,1)S(1)} collective-permute-done((bf16[256,2048]{1,0:T(8,128)(2,1)}, bf16[256,2048]{1,0:T(8,128)(2,1)S(1)}, u32[]{:S(2)}, u32[]{:S(2)}) %collective-permute-start.3) | collective-permute-done | bytes 1048608 | tf_op jit(solution)/shard_map/ppermute | solution.py:178
  59.2 1.0 copy-done
  60.1 0.0 all-gather.8.cloned.1.call-update
  60.2 0.0 copy-start.2
  60.2 0.0 all-gather.6.cloned.1.call-start
  60.2 0.7 all-gather.6.cloned.1.call-update
  60.9 0.0 all-gather.4.cloned.1.call-start
  61.0 0.0 copy-done.3
  61.0 0.1 copy.19
  61.1 0.1 reduce
  61.3 0.1 fusion.4
  61.4 0.3 reduce-window.21
  61.7 0.1 slice.10
  61.8 0.1 slice_reduce_fusion
  62.0 0.1 add_bitcast_fusion
  62.0 0.6 slice.12
  62.6 0.1 copy.17
  62.7 0.1 broadcast_in_dim.15
  62.8 1.3 compare_convert_fusion
  64.1 1.3 broadcast_in_dim.32.rates
  65.4 10.4 %shard_map.120 = f32[16,2048]{1,0:T(8,128)} custom-call(bf16[256,2048]{1,0:T(8,128)(2,1)} %key.5, bf16[256,2048]{1,0:T(8,128)(2,1)} %value.5, f32[2048,128]{1,0:T(8,128)} %broadcast_in_dim.32.rates, f32[1,256]{1,0:T(1,128)} %bitcast.18), custom_call_target="tpu_custom_call" | custom-call | flops 536870912 | bytes 3146752 | tf_op jit(solution)/shard_map/pallas_call | solution.py:144
  75.8 3.4 collective-permute-start
  79.2 2.0 collective-permute-start.1
  81.2 0.1 reduce_max.9
  81.3 0.6 fusion.5
  83.1 0.0 copy-done.2
  83.2 0.3 broadcast_in_dim.35
  83.5 0.6 mul.59
  84.1 0.1 copy.18
  84.2 0.1 broadcast_in_dim.33
  84.3 0.9 fusion.3
  85.2 0.0 collective-permute-done
  85.2 0.0 collective-permute-done.1
  85.2 0.7 multiply_add_fusion.1.state
  85.9 1.3 broadcast_in_dim.34.coeffs
  87.2 17.8 %shard_map.121 = (f32[256,2048]{1,0:T(8,128)}, bf16[256,2048]{1,0:T(8,128)(2,1)}) custom-call(bf16[256,2048]{1,0:T(8,128)(2,1)} %key.5, bf16[256,2048]{1,0:T(8,128)(2,1)} %value.5, bf16[256,2048]{1,0:T(8,128)(2,1)} %query.3, f32[1,2048]{1,0:T(1,128)} %bitcast.24, f32[2048,128]{1,0:T(8,128)} %broadcast_in_dim.32.rates, f32[2048,128]{1,0:T(8,128)} %broadcast_in_dim.34.coeffs, ...), custom_call_target="tpu_custom_call" | custom-call | flops 8589934592 | bytes 5645312 | tf_op jit(solution)/shard_map/pallas_call | solution.py:144
  105.0 0.0 all-gather.4.cloned.1.call-update
  105.0 0.0 reduce-scatter.5.cloned.1.call-start
  105.1 0.0 all-gather.8.cloned.1.call-done
  105.1 93.9 %all-gather.6.cloned.1.call-done = bf16[2048,2048]{1,0:T(8,128)(2,1)} async-done(((bf16[2048,1024]{1,0:T(8,128)(2,1)}), bf16[2048,2048]{1,0:T(8,128)(2,1)}) %all-gather.6.cloned.1.call-update) | async-done | bytes 8388624 | tf_op jit(solution)/shard_map/all_gather | solution.py:180
  199.0 13.9 %convolution_convert_fusion = bf16[1024,2048]{1,0:T(8,128)(2,1)} fusion(bf16[1024,2048]{1,0:T(8,128)(2,1)} %all-gather.8.cloned.1.call-done, bf16[2048,2048]{1,0:T(8,128)(2,1)} %all-gather.6.cloned.1.call-done), kind=kOutput, calls=%fused_computation | convolution fusion | flops 8592031744 | bytes 16777216 | tf_op jit(solution)/shard_map/dot_general | solution.py:230
  212.9 0.0 reduce-scatter.5.cloned.1.call-update
  212.9 0.0 reduce-scatter.3.cloned.1.call-start
  213.0 69.0 %all-gather.4.cloned.1.call-done = bf16[1024,2048]{1,0:T(8,128)(2,1)} async-done(((bf16[256,2048]{1,0:T(8,128)(2,1)}), bf16[1024,2048]{1,0:T(8,128)(2,1)}) %all-gather.4.cloned.1.call-update) | async-done | bytes 4194320 | tf_op jit(solution)/shard_map/all_gather | solution.py:228
  282.0 13.8 %convolution_convert_fusion.1 = bf16[1024,2048]{1,0:T(8,128)(2,1)} fusion(bf16[1024,2048]{1,0:T(8,128)(2,1)} %all-gather.4.cloned.1.call-done, bf16[2048,2048]{1,0:T(8,128)(2,1)} %all-gather.6.cloned.1.call-done), kind=kOutput, calls=%fused_computation.1 | convolution fusion | flops 8592031744 | bytes 16777216 | tf_op jit(solution)/shard_map/dot_general | solution.py:234
  295.8 0.0 reduce-scatter.3.cloned.1.call-update
  295.8 63.6 %reduce-scatter.5.cloned.1.call-done.grad = bf16[256,2048]{1,0:T(8,128)(2,1)} async-done(((bf16[1024,2048]{1,0:T(8,128)(2,1)}), bf16[256,2048]{1,0:T(8,128)(2,1)}) %reduce-scatter.5.cloned.1.call-update) | async-done | bytes 1048592 | tf_op jit(solution)/shard_map/reduce_scatter | solution.py:233
  359.4 11.3 %shard_map.122 = (bf16[256,2048]{1,0:T(8,128)(2,1)}, bf16[256,2048]{1,0:T(8,128)(2,1)}, f32[16,2048]{1,0:T(8,128)}) custom-call(bf16[256,2048]{1,0:T(8,128)(2,1)} %reduce-scatter.5.cloned.1.call-done.grad, bf16[256,2048]{1,0:T(8,128)(2,1)} %query.3, f32[256,2048]{1,0:T(8,128)} %get-tuple-element.12.mixed, f32[2048,128]{1,0:T(8,128)} %broadcast_in_dim.32.rates, ...), custom_call_target="tpu_custom_call" | custom-call | flops 536870912 | bytes 6292480 | tf_op jit(solution)/shard_map/pallas_call | solution.py:144
  370.7 1.3 collective-permute-start.4
  372.0 1.3 collective-permute-start.5
  373.3 0.3 broadcast_in_dim.36
  373.6 0.6 mul.64
  374.3 31.5 %reduce-scatter.3.cloned.1.call-done = bf16[256,2048]{1,0:T(8,128)(2,1)} async-done(((bf16[1024,2048]{1,0:T(8,128)(2,1)}), bf16[256,2048]{1,0:T(8,128)(2,1)}) %reduce-scatter.3.cloned.1.call-update) | async-done | bytes 1048592 | tf_op jit(solution)/shard_map/reduce_scatter | solution.py:235
  405.8 5.4 %collective-permute-start.2 = (bf16[256,2048]{1,0:T(8,128)(2,1)}, bf16[256,2048]{1,0:T(8,128)(2,1)S(1)}, u32[]{:S(2)}, u32[]{:S(2)}) collective-permute-start(bf16[256,2048]{1,0:T(8,128)(2,1)} %reduce-scatter.3.cloned.1.call-done), channel_id=1, source_target_pairs={{0,0},{1,8},{2,16},{3,24},{4,4},{5,12},{6,20},{7,28},{8,1},{9,9},{... | collective-permute-start | bytes 3145736 | tf_op jit(solution)/shard_map/ppermute | solution.py:236
  411.2 0.0 collective-permute-done.4
  411.2 0.0 collective-permute-done.5
  411.2 0.7 multiply_add_fusion.state
  411.9 17.4 %shard_map.123 = (bf16[256,2048]{1,0:T(8,128)(2,1)}, bf16[256,2048]{1,0:T(8,128)(2,1)}) custom-call(bf16[256,2048]{1,0:T(8,128)(2,1)} %get-tuple-element.14.grad, bf16[256,2048]{1,0:T(8,128)(2,1)} %key.5, bf16[256,2048]{1,0:T(8,128)(2,1)} %value.5, f32[1,2048]{1,0:T(1,128)} %bitcast.25, f32[2048,128]{1,0:T(8,128)} %broadcast_in_dim.32.rates, ...), custom_call_target="tpu_custom_call" | custom-call | flops 8589934592 | bytes 5645312 | tf_op jit(solution)/shard_map/pallas_call | solution.py:144
  429.3 28.5 %collective-permute-done.2 = bf16[256,2048]{1,0:T(8,128)(2,1)S(1)} collective-permute-done((bf16[256,2048]{1,0:T(8,128)(2,1)}, bf16[256,2048]{1,0:T(8,128)(2,1)S(1)}, u32[]{:S(2)}, u32[]{:S(2)}) %collective-permute-start.2) | collective-permute-done | bytes 1048608 | tf_op jit(solution)/shard_map/ppermute | solution.py:236
  457.8 1.0 copy.21
  (9 shorter events, 0.1 us)
Async XLA Ops:
  7.2 53.8 %copy-start.3 = (s32[24]{0:T(128)S(1)}, s32[24]{0:T(128)}, u32[]{:S(2)}) copy-start(s32[24]{0:T(128)} %param.17) | copy-start | bytes 292
  7.2 55.4 %copy-start.1 = (f32[128,16]{0,1:T(8,128)S(1)}, f32[128,16]{0,1:T(8,128)}, u32[]{:S(2)}) copy-start(f32[128,16]{0,1:T(8,128)} %param.15) | copy-start | bytes 24580
  7.2 97.9 %all-gather.8.cloned.1.call-start = ((), (), s32[]{:S(2)}) async-start(), calls=%async_computation.5 | async-start | bytes 5242880 | tf_op jit(solution)/shard_map/all_gather | solution.py:179
  7.2 51.9 %collective-permute-start.3 = (bf16[256,2048]{1,0:T(8,128)(2,1)}, bf16[256,2048]{1,0:T(8,128)(2,1)S(1)}, u32[]{:S(2)}, u32[]{:S(2)}) collective-permute-start(bf16[256,2048]{1,0:T(8,128)(2,1)} %param.12), channel_id=1, source_target_pairs={{0,0},{1,8},{2,16},{3,24},{4,4},{5,12},{6,20},{7,28},{8,1},{9,9},{... | collective-permute-start | bytes 3145736 | tf_op jit(solution)/shard_map/ppermute | solution.py:178
  59.2 1.0 copy-start
  60.2 23.0 %copy-start.2 = (f32[128,16]{0,1:T(8,128)S(1)}, f32[128,16]{0,1:T(8,128)}, u32[]{:S(2)}) copy-start(f32[128,16]{0,1:T(8,128)} %param.14) | copy-start | bytes 24580
  60.2 138.9 %all-gather.6.cloned.1.call-start = ((), (), s32[]{:S(2)}) async-start(), calls=%async_computation.3 | async-start | bytes 12582912 | tf_op jit(solution)/shard_map/all_gather | solution.py:180
  60.9 221.0 %all-gather.4.cloned.1.call-start = ((), (), s32[]{:S(2)}) async-start(), calls=%async_computation.2 | async-start | bytes 5242880 | tf_op jit(solution)/shard_map/all_gather | solution.py:228
  75.8 9.4 %collective-permute-start = (f32[16,2048]{1,0:T(8,128)}, f32[16,2048]{1,0:T(8,128)S(1)}, u32[]{:S(2)}, u32[]{:S(2)}) collective-permute-start(f32[16,2048]{1,0:T(8,128)} %shard_map.120), channel_id=1, source_target_pairs={{0,4},{4,8},{8,12},{12,16},{16,20},{20,24},{24,28},{1,5},{5,9},{9,... | collective-permute-start | bytes 393224 | tf_op jit(solution)/shard_map/ppermute | solution.py:210
  79.2 6.0 %collective-permute-start.1 = (f32[16,2048]{1,0:T(8,128)}, f32[16,2048]{1,0:T(8,128)S(1)}, u32[]{:S(2)}, u32[]{:S(2)}) collective-permute-start(f32[16,2048]{1,0:T(8,128)} %shard_map.120), channel_id=1, source_target_pairs={{0,8},{4,12},{8,16},{12,20},{16,24},{20,28},{1,9},{5,13},{9,17},{1... | collective-permute-start | bytes 393224 | tf_op jit(solution)/shard_map/ppermute | solution.py:210
  105.0 254.4 %reduce-scatter.5.cloned.1.call-start = ((), (), s32[]{:S(2)}) async-start(), calls=%async_computation.6 | async-start | bytes 5242880 | tf_op jit(solution)/shard_map/reduce_scatter | solution.py:233
  212.9 192.8 %reduce-scatter.3.cloned.1.call-start = ((), (), s32[]{:S(2)}) async-start(), calls=%async_computation.4 | async-start | bytes 5242880 | tf_op jit(solution)/shard_map/reduce_scatter | solution.py:235
  370.7 40.5 %collective-permute-start.4 = (f32[16,2048]{1,0:T(8,128)}, f32[16,2048]{1,0:T(8,128)S(1)}, u32[]{:S(2)}, u32[]{:S(2)}) collective-permute-start(f32[16,2048]{1,0:T(8,128)} %get-tuple-element.15), channel_id=1, source_target_pairs={{4,0},{8,4},{12,8},{16,12},{20,16},{24,20},{28,24},{5,1},{9,5},{13... | collective-permute-start | bytes 393224 | tf_op jit(solution)/shard_map/ppermute | solution.py:210
  372.0 39.2 %collective-permute-start.5 = (f32[16,2048]{1,0:T(8,128)}, f32[16,2048]{1,0:T(8,128)S(1)}, u32[]{:S(2)}, u32[]{:S(2)}) collective-permute-start(f32[16,2048]{1,0:T(8,128)} %get-tuple-element.15), channel_id=1, source_target_pairs={{8,0},{12,4},{16,8},{20,12},{24,16},{28,20},{9,1},{13,5},{17,9},{2... | collective-permute-start | bytes 393224 | tf_op jit(solution)/shard_map/ppermute | solution.py:210
  405.8 52.1 %collective-permute-start.2 = (bf16[256,2048]{1,0:T(8,128)(2,1)}, bf16[256,2048]{1,0:T(8,128)(2,1)S(1)}, u32[]{:S(2)}, u32[]{:S(2)}) collective-permute-start(bf16[256,2048]{1,0:T(8,128)(2,1)} %reduce-scatter.3.cloned.1.call-done), channel_id=1, source_target_pairs={{0,0},{1,8},{2,16},{3,24},{4,4},{5,12},{6,20},{7,28},{8,1},{9,9},{... | collective-permute-start | bytes 3145736 | tf_op jit(solution)/shard_map/ppermute | solution.py:236
Sparse Core Ops, SparseCore 0:
  60.3 32.0 all-gather.7
  93.9 105.0 all-gather.5
  201.2 80.7 all-gather.3
  284.1 75.2 reduce-scatter.4
  361.8 43.9 reduce-scatter.2

commit v2 on v1

--- a/solution.py
+++ b/solution.py
@@ -177,7 +177,14 @@
     ]
     cot = lax.ppermute(out_cotangent, ("z", "x", "tp"), transposed)
     cot_all = lax.all_gather(cot, "tp", axis=0, tiled=True)
-    weight = lax.all_gather(out_weight, "x", axis=1, tiled=True)
+    depth, width = out_weight.shape
+    weight = jnp.zeros((depth, nx * width), out_weight.dtype)
+    for shift in range(nx):
+        block = out_weight
+        if shift:
+            block = lax.ppermute(out_weight, "x", [(x, (x + shift) % nx) for x in range(nx)])
+        owner = lax.rem(lax.axis_index("x") - shift + nx, nx)
+        weight = lax.dynamic_update_slice_in_dim(weight, block, owner * width, 1)
 
     offsets = jnp.cumsum(record_lengths) - record_lengths
     everywhere = jnp.arange(length * ctx, dtype=jnp.int32)

time: 469 us -> 377 us (0.80)
  waiting for transfers between devices: 335 us -> 229 us
  local copies, waits for them, and re-layouts: 8.31 us -> 21.2 us
    all_gather x1 -> x0, waiting for transfers between devices: 93.9 us -> none  [on_device(): weight = lax.all_gather(out_weight, 'x', axis=1, tiled=True)]
    all_gather x1, waiting for transfers between devices: 69 us -> 0.02 us  [on_device(): mixer_all = lax.all_gather(mixer_out, 'z', axis=0, tiled=True)]
    ppermute x0 -> x1, waiting for transfers between devices: none -> 60.5 us  [on_device(): lax.ppermute(out_weight, 'x', [(x, (x + shift) % nx) for x in range(nx)])]
    dynamic_update_slice x0 -> x2, local copies, waits for them, and re-layouts: none -> 7.16 us  [on_device(): weight = lax.dynamic_update_slice_in_dim(weight, block, owner * width, 1)]
  transfers between devices with their start and end apart: 11 -> 11, of which waited for: 6 -> 5; matrix products, arithmetic and copies ran while one was open for 8% -> 14% of each run, Pallas kernels for 12% -> 15%
where the time goes in v2:
time: 377 us; the launch traced here: 374 us
  waiting for transfers between devices  229 us (61%)
  Pallas kernels  56.7 us (15%)
  matrix products  27.7 us (7%)
  local copies, waits for them, and re-layouts  21.2 us (6%)
  starting transfers between devices  18.3 us (5%)
  between operations  15.2 us (4%)
  other arithmetic  5.06 us (1%)
    reduce_scatter x1, waiting for transfers between devices, on_device(): mixer_grad = lax.psum_scatter(back, 'z', scatter_dimension=0, tiled=True)  61.3 us
    ppermute x1, waiting for transfers between devices, on_device(): lax.ppermute(out_weight, 'x', [(x, (x + shift) % nx) for x in range(nx)])  60.5 us
    pallas_call x4, Pallas kernels, tiled_call(): pl.pallas_call(functools.partial(body, modes), grid=(channels // LANES,),...  56.7 us
    ppermute x1, waiting for transfers between devices, on_device(): cot = lax.ppermute(out_cotangent, ('z', 'x', 'tp'), transposed)  47.5 us
    reduce_scatter x1, waiting for transfers between devices, on_device(): summed = lax.psum_scatter(partial, 'tp', scatter_dimension=0, tiled=True)  31.6 us
    ppermute x1, waiting for transfers between devices, on_device(): block_output = lax.ppermute(summed, ('z', 'x', 'tp'), transposed)  28.5 us
    dot_general x1, matrix products, on_device(): lax.dot_general(cot_all, weight, (((1,), (1,)), ((), ())), preferred_elem...  13.9 us
    dot_general x1, matrix products, on_device(): jnp.dot(mixer_all, weight, preferred_element_type=F32).astype(BF16)  13.8 us
  transfers between devices with their start and end apart: 11, of which 5 were waited for; matrix products, arithmetic and copies ran while one was open for 14% of the time, Pallas kernels for 15%

profile of v2, /device:TPU:4, one launch (start us, length us, event | category | flops | bytes accessed | tf_op | source)
XLA Modules:
  0.0 373.5 jit_solution(2042116529933840030)
XLA Ops:
  7.2 0.0 copy-start.2
  7.2 0.0 copy-start.3
  7.2 0.0 all-gather.5.cloned.1.call-start
  7.2 4.4 %collective-permute-start.4 = (bf16[256,2048]{1,0:T(8,128)(2,1)}, bf16[256,2048]{1,0:T(8,128)(2,1)S(1)}, u32[]{:S(2)}, u32[]{:S(2)}) collective-permute-start(bf16[256,2048]{1,0:T(8,128)(2,1)} %param.12), channel_id=1, source_target_pairs={{0,0},{1,8},{2,16},{3,24},{4,4},{5,12},{6,20},{7,28},{8,1},{9,9},{... | collective-permute-start | bytes 3145736 | tf_op jit(solution)/shard_map/ppermute | solution.py:178
  11.7 47.5 %collective-permute-done.4 = bf16[256,2048]{1,0:T(8,128)(2,1)S(1)} collective-permute-done((bf16[256,2048]{1,0:T(8,128)(2,1)}, bf16[256,2048]{1,0:T(8,128)(2,1)S(1)}, u32[]{:S(2)}, u32[]{:S(2)}) %collective-permute-start.4) | collective-permute-done | bytes 1048608 | tf_op jit(solution)/shard_map/ppermute | solution.py:178
  59.2 1.0 copy-done.1
  60.1 0.0 all-gather.5.cloned.1.call-update
  60.2 0.0 all-gather.3.cloned.1.call-start
  60.2 0.7 copy.21
  61.0 0.1 reduce
  61.1 0.7 sub.30
  61.8 0.1 fusion.4
  61.9 0.3 reduce-window.21
  62.3 0.1 slice.10
  62.4 0.1 slice_reduce_fusion
  62.5 0.1 add_bitcast_fusion
  62.6 0.6 slice.12
  63.1 0.8 copy.19
  63.9 0.1 broadcast_in_dim.34
  64.0 1.3 compare_convert_fusion
  65.3 1.3 broadcast_in_dim.35.rates
  66.6 10.4 %shard_map.120 = f32[16,2048]{1,0:T(8,128)} custom-call(bf16[256,2048]{1,0:T(8,128)(2,1)} %key.5, bf16[256,2048]{1,0:T(8,128)(2,1)} %value.5, f32[2048,128]{1,0:T(8,128)} %broadcast_in_dim.35.rates, f32[1,256]{1,0:T(1,128)} %bitcast.20), custom_call_target="tpu_custom_call" | custom-call | flops 536870912 | bytes 3146752 | tf_op jit(solution)/shard_map/pallas_call | solution.py:144
  77.0 3.4 collective-permute-start
  80.4 2.1 collective-permute-start.1
  82.5 0.1 collective-permute-start.2
  82.6 0.1 reduce_max.9
  82.7 0.6 fusion.5
  84.6 0.3 broadcast_in_dim.38
  84.9 0.6 mul.65
  85.6 0.1 copy.20
  85.7 0.1 broadcast_in_dim.36
  85.7 0.9 fusion.3
  86.7 0.0 collective-permute-done
  86.7 0.0 collective-permute-done.1
  86.7 0.7 multiply_add_fusion.1.state
  87.3 1.3 broadcast_in_dim.37.coeffs
  88.7 17.6 %shard_map.121 = (f32[256,2048]{1,0:T(8,128)}, bf16[256,2048]{1,0:T(8,128)(2,1)}) custom-call(bf16[256,2048]{1,0:T(8,128)(2,1)} %key.5, bf16[256,2048]{1,0:T(8,128)(2,1)} %value.5, bf16[256,2048]{1,0:T(8,128)(2,1)} %query.3, f32[1,2048]{1,0:T(1,128)} %bitcast.26, f32[2048,128]{1,0:T(8,128)} %broadcast_in_dim.35.rates, f32[2048,128]{1,0:T(8,128)} %broadcast_in_dim.37.coeffs, ...), custom_call_target="tpu_custom_call" | custom-call | flops 8589934592 | bytes 5645312 | tf_op jit(solution)/shard_map/pallas_call | solution.py:144
  106.3 0.0 all-gather.3.cloned.1.call-update
  106.3 0.0 reduce-scatter.5.cloned.1.call-start
  106.4 0.0 copy-start
  106.4 4.3 %broadcast_in_dim.39 = bf16[2048,2048]{1,0:T(8,128)(2,1)} broadcast(bf16[]{:T(256)} %constant.59.clone.1), dimensions={} | broadcast | bytes 8388610 | tf_op jit(solution)/shard_map/broadcast_in_dim | solution.py:181
  110.7 2.4 constant_dynamic-update-slice_fusion.1
  113.1 60.5 %collective-permute-done.2 = bf16[2048,1024]{1,0:T(8,128)(2,1)} collective-permute-done((bf16[2048,1024]{1,0:T(8,128)(2,1)}, bf16[2048,1024]{1,0:T(8,128)(2,1)}, u32[]{:S(2)}, u32[]{:S(2)}) %collective-permute-start.2) | collective-permute-done | bytes 4194336 | tf_op jit(solution)/shard_map/ppermute | solution.py:185
  173.6 4.7 %constant_dynamic-update-slice_fusion = bf16[2048,2048]{1,0:T(8,128)(2,1)} fusion(bf16[2048,2048]{1,0:T(8,128)(2,1)} %constant_dynamic-update-slice_fusion.1, bf16[2048,1024]{1,0:T(8,128)(2,1)} %collective-permute-done.2, s32[]{:T(128)S(6)} %select_n.14), kind=kLoop, calls=%fused_computation.19 | loop fusion | bytes 8388612 | tf_op jit(solution)/shard_map/dynamic_update_slice | solution.py:187
  178.3 13.9 %convert_bitcast_fusion = bf16[1024,2048]{1,0:T(8,128)(2,1)} fusion(bf16[2048,2048]{1,0:T(8,128)(2,1)} %constant_dynamic-update-slice_fusion, bf16[1024,2048]{1,0:T(8,128)(2,1)} %all-gather.5.cloned.1.call-done), kind=kOutput, calls=%fused_computation | convolution fusion | flops 8592031744 | bytes 16777216 | tf_op jit(solution)/shard_map/dot_general | solution.py:237
  192.2 0.0 reduce-scatter.5.cloned.1.call-update
  192.2 0.2 reduce-scatter.3.cloned.1.call-start
  192.4 0.0 all-gather.3.cloned.1.call-done
  192.4 13.8 %convolution_convert_fusion = bf16[1024,2048]{1,0:T(8,128)(2,1)} fusion(bf16[1024,2048]{1,0:T(8,128)(2,1)} %all-gather.3.cloned.1.call-done, bf16[2048,2048]{1,0:T(8,128)(2,1)} %constant_dynamic-update-slice_fusion), kind=kOutput, calls=%fused_computation.1 | convolution fusion | flops 8592031744 | bytes 16777216 | tf_op jit(solution)/shard_map/dot_general | solution.py:241
  206.3 0.0 reduce-scatter.3.cloned.1.call-update
  206.3 61.3 %reduce-scatter.5.cloned.1.call-done.grad = bf16[256,2048]{1,0:T(8,128)(2,1)} async-done(((bf16[1024,2048]{1,0:T(8,128)(2,1)}), bf16[256,2048]{1,0:T(8,128)(2,1)}) %reduce-scatter.5.cloned.1.call-update) | async-done | bytes 1048592 | tf_op jit(solution)/shard_map/reduce_scatter | solution.py:240
  267.6 11.3 %shard_map.122 = (bf16[256,2048]{1,0:T(8,128)(2,1)}, bf16[256,2048]{1,0:T(8,128)(2,1)}, f32[16,2048]{1,0:T(8,128)}) custom-call(bf16[256,2048]{1,0:T(8,128)(2,1)} %reduce-scatter.5.cloned.1.call-done.grad, bf16[256,2048]{1,0:T(8,128)(2,1)} %query.3, f32[256,2048]{1,0:T(8,128)} %get-tuple-element.12.mixed, f32[2048,128]{1,0:T(8,128)} %broadcast_in_dim.35.rates, ...), custom_call_target="tpu_custom_call" | custom-call | flops 536870912 | bytes 6292480 | tf_op jit(solution)/shard_map/pallas_call | solution.py:144
  278.9 1.3 collective-permute-start.5
  280.2 1.3 collective-permute-start.6
  281.5 0.3 broadcast_in_dim.40
  281.8 0.6 mul.72
  282.4 31.6 %reduce-scatter.3.cloned.1.call-done = bf16[256,2048]{1,0:T(8,128)(2,1)} async-done(((bf16[1024,2048]{1,0:T(8,128)(2,1)}), bf16[256,2048]{1,0:T(8,128)(2,1)}) %reduce-scatter.3.cloned.1.call-update) | async-done | bytes 1048592 | tf_op jit(solution)/shard_map/reduce_scatter | solution.py:242
  314.0 5.4 %collective-permute-start.3 = (bf16[256,2048]{1,0:T(8,128)(2,1)}, bf16[256,2048]{1,0:T(8,128)(2,1)S(1)}, u32[]{:S(2)}, u32[]{:S(2)}) collective-permute-start(bf16[256,2048]{1,0:T(8,128)(2,1)} %reduce-scatter.3.cloned.1.call-done), channel_id=1, source_target_pairs={{0,0},{1,8},{2,16},{3,24},{4,4},{5,12},{6,20},{7,28},{8,1},{9,9},{... | collective-permute-start | bytes 3145736 | tf_op jit(solution)/shard_map/ppermute | solution.py:243
  319.4 0.0 collective-permute-done.5
  319.4 0.0 collective-permute-done.6
  319.4 0.7 multiply_add_fusion.state
  320.1 17.4 %shard_map.123 = (bf16[256,2048]{1,0:T(8,128)(2,1)}, bf16[256,2048]{1,0:T(8,128)(2,1)}) custom-call(bf16[256,2048]{1,0:T(8,128)(2,1)} %get-tuple-element.14.grad, bf16[256,2048]{1,0:T(8,128)(2,1)} %key.5, bf16[256,2048]{1,0:T(8,128)(2,1)} %value.5, f32[1,2048]{1,0:T(1,128)} %bitcast.27, f32[2048,128]{1,0:T(8,128)} %broadcast_in_dim.35.rates, ...), custom_call_target="tpu_custom_call" | custom-call | flops 8589934592 | bytes 5645312 | tf_op jit(solution)/shard_map/pallas_call | solution.py:144
  337.5 28.5 %collective-permute-done.3 = bf16[256,2048]{1,0:T(8,128)(2,1)S(1)} collective-permute-done((bf16[256,2048]{1,0:T(8,128)(2,1)}, bf16[256,2048]{1,0:T(8,128)(2,1)S(1)}, u32[]{:S(2)}, u32[]{:S(2)}) %collective-permute-start.3) | collective-permute-done | bytes 1048608 | tf_op jit(solution)/shard_map/ppermute | solution.py:243
  366.0 1.0 copy.27
  (11 shorter events, 0.1 us)
Async XLA Ops:
  7.2 77.4 %copy-start.2 = (f32[128,16]{0,1:T(8,128)S(1)}, f32[128,16]{0,1:T(8,128)}, u32[]{:S(2)}) copy-start(f32[128,16]{0,1:T(8,128)} %param.15) | copy-start | bytes 24580
  7.2 77.4 %copy-start.3 = (f32[128,16]{0,1:T(8,128)S(1)}, f32[128,16]{0,1:T(8,128)}, u32[]{:S(2)}) copy-start(f32[128,16]{0,1:T(8,128)} %param.14) | copy-start | bytes 24580
  7.2 171.1 %all-gather.5.cloned.1.call-start = ((), (), s32[]{:S(2)}) async-start(), calls=%async_computation.4 | async-start | bytes 5242880 | tf_op jit(solution)/shard_map/all_gather | solution.py:179
  7.2 51.9 %collective-permute-start.4 = (bf16[256,2048]{1,0:T(8,128)(2,1)}, bf16[256,2048]{1,0:T(8,128)(2,1)S(1)}, u32[]{:S(2)}, u32[]{:S(2)}) collective-permute-start(bf16[256,2048]{1,0:T(8,128)(2,1)} %param.12), channel_id=1, source_target_pairs={{0,0},{1,8},{2,16},{3,24},{4,4},{5,12},{6,20},{7,28},{8,1},{9,9},{... | collective-permute-start | bytes 3145736 | tf_op jit(solution)/shard_map/ppermute | solution.py:178
  59.2 1.0 copy-start.1
  60.2 132.3 %all-gather.3.cloned.1.call-start = ((), (), s32[]{:S(2)}) async-start(), calls=%async_computation.2 | async-start | bytes 5242880 | tf_op jit(solution)/shard_map/all_gather | solution.py:235
  77.0 9.7 %collective-permute-start = (f32[16,2048]{1,0:T(8,128)}, f32[16,2048]{1,0:T(8,128)S(1)}, u32[]{:S(2)}, u32[]{:S(2)}) collective-permute-start(f32[16,2048]{1,0:T(8,128)} %shard_map.120), channel_id=1, source_target_pairs={{0,4},{4,8},{8,12},{12,16},{16,20},{20,24},{24,28},{1,5},{5,9},{9,... | collective-permute-start | bytes 393224 | tf_op jit(solution)/shard_map/ppermute | solution.py:217
  80.4 6.3 %collective-permute-start.1 = (f32[16,2048]{1,0:T(8,128)}, f32[16,2048]{1,0:T(8,128)S(1)}, u32[]{:S(2)}, u32[]{:S(2)}) collective-permute-start(f32[16,2048]{1,0:T(8,128)} %shard_map.120), channel_id=1, source_target_pairs={{0,8},{4,12},{8,16},{12,20},{16,24},{20,28},{1,9},{5,13},{9,17},{1... | collective-permute-start | bytes 393224 | tf_op jit(solution)/shard_map/ppermute | solution.py:217
  82.5 91.1 %collective-permute-start.2 = (bf16[2048,1024]{1,0:T(8,128)(2,1)}, bf16[2048,1024]{1,0:T(8,128)(2,1)}, u32[]{:S(2)}, u32[]{:S(2)}) collective-permute-start(bf16[2048,1024]{1,0:T(8,128)(2,1)} %param.13), channel_id=1, source_target_pairs={{0,4},{4,0},{1,5},{5,1},{2,6},{6,2},{3,7},{7,3},{8,12},{12,8},{9,1... | collective-permute-start | bytes 12582920 | tf_op jit(solution)/shard_map/ppermute | solution.py:185
  106.3 161.3 %reduce-scatter.5.cloned.1.call-start = ((), (), s32[]{:S(2)}) async-start(), calls=%async_computation.5 | async-start | bytes 5242880 | tf_op jit(solution)/shard_map/reduce_scatter | solution.py:240
  106.4 4.3 %copy-start = (bf16[2048,1024]{1,0:T(8,128)(2,1)S(1)}, bf16[2048,1024]{1,0:T(8,128)(2,1)}, u32[]{:S(2)}) copy-start(bf16[2048,1024]{1,0:T(8,128)(2,1)} %param.13) | copy-start | bytes 12582916
  192.2 121.8 %reduce-scatter.3.cloned.1.call-start = ((), (), s32[]{:S(2)}) async-start(), calls=%async_computation.3 | async-start | bytes 5242880 | tf_op jit(solution)/shard_map/reduce_scatter | solution.py:242
  278.9 40.5 %collective-permute-start.5 = (f32[16,2048]{1,0:T(8,128)}, f32[16,2048]{1,0:T(8,128)S(1)}, u32[]{:S(2)}, u32[]{:S(2)}) collective-permute-start(f32[16,2048]{1,0:T(8,128)} %get-tuple-element.15), channel_id=1, source_target_pairs={{4,0},{8,4},{12,8},{16,12},{20,16},{24,20},{28,24},{5,1},{9,5},{13... | collective-permute-start | bytes 393224 | tf_op jit(solution)/shard_map/ppermute | solution.py:217
  280.2 39.2 %collective-permute-start.6 = (f32[16,2048]{1,0:T(8,128)}, f32[16,2048]{1,0:T(8,128)S(1)}, u32[]{:S(2)}, u32[]{:S(2)}) collective-permute-start(f32[16,2048]{1,0:T(8,128)} %get-tuple-element.15), channel_id=1, source_target_pairs={{8,0},{12,4},{16,8},{20,12},{24,16},{28,20},{9,1},{13,5},{17,9},{2... | collective-permute-start | bytes 393224 | tf_op jit(solution)/shard_map/ppermute | solution.py:217
  314.0 52.0 %collective-permute-start.3 = (bf16[256,2048]{1,0:T(8,128)(2,1)}, bf16[256,2048]{1,0:T(8,128)(2,1)S(1)}, u32[]{:S(2)}, u32[]{:S(2)}) collective-permute-start(bf16[256,2048]{1,0:T(8,128)(2,1)} %reduce-scatter.3.cloned.1.call-done), channel_id=1, source_target_pairs={{0,0},{1,8},{2,16},{3,24},{4,4},{5,12},{6,20},{7,28},{8,1},{9,9},{... | collective-permute-start | bytes 3145736 | tf_op jit(solution)/shard_map/ppermute | solution.py:243
Sparse Core Ops, SparseCore 0:
  60.3 32.0 all-gather.4
  106.4 79.5 all-gather.2
  192.3 75.2 reduce-scatter.4
  270.0 43.9 reduce-scatter.2
